TPU v7x, 32 devices: a whole 2x2x4 slice. The times are simulated.
32 devices in a mesh: seg: 8 (over y, x, core), head: 4 (over z).
Axes of the slice: x: 2, y: 2, z: 4, core: 2. Of those that a mesh axis runs over, the one named last changes fastest.
Arguments:
- layer_input: bfloat16 [1, 4096, 2048], P(None, 'seg', 'head'), may hold values from -160 to 160, as said below
- w_qkv: bfloat16 [2048, 3, 1024], P(None, None, 'head'), may hold values from -3 to 3
- comp_weight: bfloat16 [3, 2, 1024], P(None, None, 'head'), may hold values from -2.5 to 2.5
- w_out: bfloat16 [1024, 2048], P('seg', 'head'), may hold values from -1.5 to 1.5
Outputs:
- attn_out: bfloat16 [1, 4096, 2048], P(None, 'seg', 'head')
Inputs may be any that keep to these rules, and one draw needn't show every extreme that they name: layer_input varies in scale from feature to feature and from token to token.
All inputs are finite; a program needn't handle non-finite values.
Results may differ from a plain program's by a relative error of at most 0.0089.
Values may be sent and summed in bfloat16 or wider, within the bound.
No kernel may reach another device: no remote copies, remote signals or barrier semaphores. Data moves between devices by JAX's collectives and lax.ppermute only.
A program may use at most 64 MiB of HBM per device.

v0:
```python
import math
import jax
import jax.numpy as jnp
from jax import lax
from jax.sharding import PartitionSpec as P

DH = 128


def passed_along(block, axis, distance):
    devices = range(lax.axis_size(axis))
    route = [(i - distance, i) for i in devices if i - distance in devices]
    return lax.ppermute(block, axis, route)


def layer_norm(values):
    center_mean = jnp.mean(values, axis=-1, keepdims=True)
    centered = values - center_mean
    variance = jnp.mean(centered * centered, axis=-1, keepdims=True)
    return centered * lax.rsqrt(variance + 1e-05)


def compress_block(source, weight):
    batch, pair, length, width = source.shape
    grouped = source.reshape(batch, pair, length // 3, 3, width)
    mixed = jnp.einsum("bkltc,tkc->bklc", grouped, weight, preferred_element_type=jnp.float32)
    return mixed.astype(jnp.bfloat16)


def key_allowed(seg_len, segment):
    query_pos = jnp.arange(seg_len)[:, None]
    key_pos = jnp.arange(3 * seg_len)[None, :]
    own_part = (key_pos >= 2 * seg_len) & (key_pos - 2 * seg_len <= query_pos)
    memory_part = (key_pos >= seg_len) & (key_pos < 2 * seg_len) & (segment >= 1)
    comp_part = (key_pos < seg_len) & (segment >= 4)
    return own_part | memory_part | comp_part


def attend(queries, key_vals, segment):
    batch, seg_len, width = queries.shape
    heads_here = width // DH
    query_heads = queries.reshape(batch, seg_len, heads_here, DH)
    key_heads = key_vals[:, 0].reshape(batch, 3 * seg_len, heads_here, DH)
    value_heads = key_vals[:, 1].reshape(batch, 3 * seg_len, heads_here, DH)
    scores = jnp.einsum(
        "bqhd,bkhd->bhqk", query_heads, key_heads, preferred_element_type=jnp.float32
    )
    scores = scores / math.sqrt(DH)
    allowed = key_allowed(seg_len, segment)
    scores = jnp.where(allowed[None, None], scores, jnp.float32(-1e30))
    highest = jnp.max(scores, axis=-1, keepdims=True)
    exponent = jnp.exp(scores - highest)
    weights = (exponent / jnp.sum(exponent, axis=-1, keepdims=True)).astype(jnp.bfloat16)
    mixed = jnp.einsum("bhqk,bkhd->bqhd", weights, value_heads, preferred_element_type=jnp.float32)
    return mixed.astype(jnp.bfloat16).reshape(batch, seg_len, width)


def local(layer_input, w_qkv, comp_weight, w_out):
    gathered = lax.all_gather(layer_input, "head", axis=2, tiled=True)
    normed = layer_norm(gathered.astype(jnp.float32)).astype(jnp.bfloat16)
    projected = jnp.einsum("bld,dkc->bklc", normed, w_qkv, preferred_element_type=jnp.float32)
    projected = projected.astype(jnp.bfloat16)
    queries = projected[:, 0]
    key_vals = projected[:, 1:3]
    memory = passed_along(key_vals, "seg", 1)
    second_back = passed_along(memory, "seg", 1)
    upcoming = compress_block(jnp.concatenate([second_back, memory, key_vals], axis=2), comp_weight)
    compressed = passed_along(upcoming, "seg", 2)
    segment = lax.axis_index("seg")
    joined = jnp.concatenate([compressed, memory, key_vals], axis=2)
    context = attend(queries, joined, segment)
    full_ctx = lax.all_gather(context, "head", axis=2, tiled=True)
    whole_out = lax.all_gather(w_out, "seg", axis=0, tiled=True)
    result_sum = jnp.einsum("blr,rc->blc", full_ctx, whole_out, preferred_element_type=jnp.float32)
    return result_sum.astype(jnp.bfloat16)


def solution(mesh):
    return jax.shard_map(
        local,
        mesh=mesh,
        in_specs=(
            P(None, "seg", "head"),
            P(None, None, "head"),
            P(None, None, "head"),
            P("seg", "head"),
        ),
        out_specs=P(None, "seg", "head"),
        check_vma=False,
    )
```

profile of v0, /device:TPU:0, one launch (start us, length us, event | category | flops | bytes accessed | tf_op | source)
XLA Modules:
  0.0 164.3 jit_solution(6512609901003673193)
XLA Ops:
  7.4 0.0 copy-start
  7.4 0.0 all-gather.4.cloned.1.call-start
  7.4 0.7 all-gather.4.cloned.1.call-update
  8.1 0.0 all-gather.8.cloned.1.call-start
  8.1 50.0 %all-gather.4.cloned.1.call-done = bf16[1,512,2048]{2,1,0:T(8,128)(2,1)} async-done(((bf16[1,512,512]{2,1,0:T(8,128)(2,1)}), bf16[1,512,2048]{2,1,0:T(8,128)(2,1)}) %all-gather.4.cloned.1.call-update) | async-done | bytes 2097168 | tf_op jit(solution)/shard_map/all_gather | solution.py:59
  58.1 0.0 copy-start.1
  58.2 2.1 %convert_reduce_fusion = f32[512]{0:T(512)S(1)} fusion(bf16[1,512,2048]{2,1,0:T(8,128)(2,1)} %all-gather.4.cloned.1.call-done), kind=kLoop, calls=%fused_computation.6 | loop fusion | flops 2096640 | bytes 2099200 | tf_op jit(solution)/shard_map/reduce_sum | solution.py:17
  60.3 0.1 copy-done.1
  60.4 0.7 fusion.4
  61.1 0.0 copy-done
  61.1 0.0 copy-start.4
  61.1 2.0 %fusion.21 = bf16[1,3,512,256]{2,3,1,0:T(8,128)(2,1)S(1)} fusion(bf16[2048,3,256]{2,0,1:T(8,128)(2,1)S(1)} %copy-done, bf16[1,512,2048]{2,1,0:T(8,128)(2,1)S(1)} %copy-done.1, f32[512]{0:T(512)S(1)} %add_rsqrt_fusion, f32[512]{0:T(512)S(1)} %broadcast_multiply_fusion), kind=kOutput, calls=%fused_computation.29 | convolution fusion | flops 1615200256 | bytes 6033408 | tf_op jit(solution)/shard_map/bld,dkc->bklc/dot_general | solution.py:61
  63.1 0.0 copy-start.3
  63.1 0.0 copy-start.2
  63.1 0.8 copy-done.2
  64.0 2.4 %collective-permute-start = (bf16[1,2,512,256]{2,3,1,0:T(8,128)(2,1)S(1)}, bf16[1,2,512,256]{2,3,1,0:T(8,128)(2,1)}, u32[]{:S(2)}, u32[]{:S(2)}) collective-permute-start(bf16[1,2,512,256]{2,3,1,0:T(8,128)(2,1)S(1)} %slice.16), channel_id=1, source_target_pairs={{0,4},{4,8},{8,12},{12,16},{16,20},{20,24},{24,28},{1,5},{5,9},{9,... | collective-permute-start | bytes 1572872 | tf_op jit(solution)/shard_map/ppermute | solution.py:13
  66.4 0.8 collective-permute-done
  67.2 0.0 copy-done.3
  67.2 9.1 %collective-permute-start.1 = (bf16[1,2,512,256]{2,3,1,0:T(8,128)(2,1)}, bf16[1,2,512,256]{2,3,1,0:T(8,128)(2,1)}, u32[]{:S(2)}, u32[]{:S(2)}) collective-permute-start(bf16[1,2,512,256]{2,3,1,0:T(8,128)(2,1)} %collective-permute-done), channel_id=1, source_target_pairs={{0,4},{4,8},{8,12},{12,16},{16,20},{20,24},{24,28},{1,5},{5,9},{9,... | collective-permute-start | bytes 1572872 | tf_op jit(solution)/shard_map/ppermute | solution.py:13
  76.3 0.0 all-gather.8.cloned.1.call-update
  76.3 0.0 all-gather.6.cloned.1.call-start
  76.4 0.0 copy-done.4
  76.4 0.9 collective-permute-done.1
  77.3 2.6 %pad_maximum_fusion.1 = bf16[1,2,1536,256]{2,3,1,0:T(8,128)(2,1)} fusion(bf16[1,2,512,256]{2,3,1,0:T(8,128)(2,1)} %copy-done.2, bf16[1,2,512,256]{2,3,1,0:T(8,128)(2,1)} %collective-permute-done, bf16[1,2,512,256]{2,3,1,0:T(8,128)(2,1)} %collective-permute-done.1), kind=kLoop, calls=%fused_computation.25 | loop fusion | flops 4718592 | bytes 3145728 | tf_op jit(solution)/shard_map/concatenate | solution.py:67
  80.0 4.9 %copy.23 = bf16[1,2,1536,256]{3,1,2,0:T(2,128)(2,1)} copy(bf16[1,2,1536,256]{2,3,1,0:T(8,128)(2,1)} %pad_maximum_fusion.1) | data formatting | bytes 3145728
  84.9 5.0 %multiply_reduce_fusion = bf16[2,256,512]{1,0,2:T(2,128)(2,1)} fusion(bf16[2,256,3,512]{1,0,2,3:T(2,128)(2,1)} %bitcast.45, f32[2,256,3]{1,0,2:T(2,128)S(1)} %bitcast_convert_fusion), kind=kLoop, calls=%fused_computation.11 | loop fusion | flops 2097152 | bytes 2103296
  89.9 2.0 %copy.20 = bf16[2,256,512]{2,1,0:T(8,128)(2,1)} copy(bf16[2,256,512]{1,0,2:T(2,128)(2,1)} %multiply_reduce_fusion) | data formatting | bytes 1048576 | tf_op jit(solution)/shard_map/bkltc,tkc->bklc/dot_general | solution.py:26
  91.9 11.8 %collective-permute-start.2 = (bf16[1,2,512,256]{2,3,1,0:T(8,128)(2,1)}, bf16[1,2,512,256]{2,3,1,0:T(8,128)(2,1)S(1)}, u32[]{:S(2)}, u32[]{:S(2)}) collective-permute-start(bf16[1,2,512,256]{2,3,1,0:T(8,128)(2,1)} %bitcast.49), channel_id=1, source_target_pairs={{0,8},{4,12},{8,16},{12,20},{16,24},{20,28},{1,9},{5,13},{9,17},{1... | collective-permute-start | bytes 1572872 | tf_op jit(solution)/shard_map/ppermute | solution.py:13
  103.7 1.6 fusion.10
  105.3 1.0 slice.18
  106.3 9.7 %collective-permute-done.2 = bf16[1,2,512,256]{2,3,1,0:T(8,128)(2,1)S(1)} collective-permute-done((bf16[1,2,512,256]{2,3,1,0:T(8,128)(2,1)}, bf16[1,2,512,256]{2,3,1,0:T(8,128)(2,1)S(1)}, u32[]{:S(2)}, u32[]{:S(2)}) %collective-permute-start.2) | collective-permute-done | bytes 524320 | tf_op jit(solution)/shard_map/ppermute | solution.py:13
  116.0 1.3 pad_maximum_fusion
  117.3 1.3 fusion.39
  118.6 3.8 %fusion.40 = f32[2,512]{1,0:T(2,128)S(1)} fusion(pred[512,1536]{1,0:T(8,128)(4,1)} %fusion.10, bf16[512,2,128]{0,2,1:T(8,128)(2,1)S(1)} %bitcast.50, bf16[1536,2,128]{0,2,1:T(8,128)(2,1)} %bitcast.46), kind=kOutput, calls=%fused_computation.53 | convolution fusion | flops 408946176 | bytes 1839104 | tf_op jit(solution)/shard_map/sub | solution.py:52
  122.5 5.2 %fusion.25 = bf16[2,128,512]{2,1,0:T(8,128)(2,1)} fusion(bf16[1536,2,128]{0,2,1:T(8,128)(2,1)} %bitcast.48, f32[2,512]{1,0:T(2,128)S(1)} %fusion.40, pred[512,1536]{1,0:T(8,128)(4,1)} %fusion.10, bf16[512,2,128]{0,2,1:T(8,128)(2,1)S(1)} %bitcast.51, bf16[1536,2,128]{0,2,1:T(8,128)(2,1)} %bitcast.47), kind=kOutput, calls=%fused_computation.32 | convolution fusion | flops 813304320 | bytes 2887680 | tf_op jit(solution)/shard_map/bhqk,bkhd->bqhd/dot_general | solution.py:54
  127.6 0.0 all-gather.6.cloned.1.call-update
  127.7 0.0 all-gather.8.cloned.1.call-done
  127.7 26.1 %all-gather.6.cloned.1.call-done = bf16[1,512,1024]{1,2,0:T(8,128)(2,1)} async-done(((bf16[1,512,256]{1,2,0:T(8,128)(2,1)}), bf16[1,512,1024]{1,2,0:T(8,128)(2,1)}) %all-gather.6.cloned.1.call-update) | async-done | bytes 1048592 | tf_op jit(solution)/shard_map/all_gather | solution.py:72
  153.8 3.1 %fusion.24 = bf16[1,512,512]{2,1,0:T(8,128)(2,1)} fusion(bf16[1024,512]{1,0:T(8,128)(2,1)} %all-gather.8.cloned.1.call-done, bf16[1,512,1024]{1,2,0:T(8,128)(2,1)} %all-gather.6.cloned.1.call-done), kind=kOutput, calls=%fused_computation.31 | convolution fusion | flops 537133056 | bytes 2621440 | tf_op jit(solution)/shard_map/blr,rc->blc/dot_general | solution.py:74
  (7 shorter events, 0.1 us)
Async XLA Ops:
  7.4 53.7 %copy-start = (bf16[2048,3,256]{2,0,1:T(8,128)(2,1)S(1)}, bf16[2048,3,256]{2,0,1:T(8,128)(2,1)}, u32[]{:S(2)}) copy-start(bf16[2048,3,256]{2,0,1:T(8,128)(2,1)} %param.5) | copy-start | bytes 9437188
  7.4 50.8 %all-gather.4.cloned.1.call-start = ((), (), s32[]{:S(2)}) async-start(), calls=%async_computation | async-start | bytes 2621440 | tf_op jit(solution)/shard_map/all_gather | solution.py:59
  8.1 119.6 %all-gather.8.cloned.1.call-start = ((), (), s32[]{:S(2)}) async-start(), calls=%async_computation.2 | async-start | bytes 1179648 | tf_op jit(solution)/shard_map/all_gather | solution.py:73
  58.1 2.2 %copy-start.1 = (bf16[1,512,2048]{2,1,0:T(8,128)(2,1)S(1)}, bf16[1,512,2048]{2,1,0:T(8,128)(2,1)}, u32[]{:S(2)}) copy-start(bf16[1,512,2048]{2,1,0:T(8,128)(2,1)} %all-gather.4.cloned.1.call-done) | copy-start | bytes 6291460
  61.1 15.3 %copy-start.4 = (bf16[3,2,256]{2,1,0:T(2,128)(2,1)S(1)}, bf16[3,2,256]{2,1,0:T(2,128)(2,1)}, u32[]{:S(2)}) copy-start(bf16[3,2,256]{2,1,0:T(2,128)(2,1)} %param.6) | copy-start | bytes 9220
  63.1 4.1 %copy-start.3 = (bf16[1,3,512,256]{2,3,1,0:T(8,128)(2,1)}, bf16[1,3,512,256]{2,3,1,0:T(8,128)(2,1)S(1)}, u32[]{:S(2)}) copy-start(bf16[1,3,512,256]{2,3,1,0:T(8,128)(2,1)S(1)} %fusion.21) | copy-start | bytes 2359300
  63.1 0.9 copy-start.2
  64.0 3.2 %collective-permute-start = (bf16[1,2,512,256]{2,3,1,0:T(8,128)(2,1)S(1)}, bf16[1,2,512,256]{2,3,1,0:T(8,128)(2,1)}, u32[]{:S(2)}, u32[]{:S(2)}) collective-permute-start(bf16[1,2,512,256]{2,3,1,0:T(8,128)(2,1)S(1)} %slice.16), channel_id=1, source_target_pairs={{0,4},{4,8},{8,12},{12,16},{16,20},{20,24},{24,28},{1,5},{5,9},{9,... | collective-permute-start | bytes 1572872 | tf_op jit(solution)/shard_map/ppermute | solution.py:13
  67.2 10.1 %collective-permute-start.1 = (bf16[1,2,512,256]{2,3,1,0:T(8,128)(2,1)}, bf16[1,2,512,256]{2,3,1,0:T(8,128)(2,1)}, u32[]{:S(2)}, u32[]{:S(2)}) collective-permute-start(bf16[1,2,512,256]{2,3,1,0:T(8,128)(2,1)} %collective-permute-done), channel_id=1, source_target_pairs={{0,4},{4,8},{8,12},{12,16},{16,20},{20,24},{24,28},{1,5},{5,9},{9,... | collective-permute-start | bytes 1572872 | tf_op jit(solution)/shard_map/ppermute | solution.py:13
  76.3 77.5 %all-gather.6.cloned.1.call-start = ((), (), s32[]{:S(2)}) async-start(), calls=%async_computation.1 | async-start | bytes 1310720 | tf_op jit(solution)/shard_map/all_gather | solution.py:72
  91.9 24.1 %collective-permute-start.2 = (bf16[1,2,512,256]{2,3,1,0:T(8,128)(2,1)}, bf16[1,2,512,256]{2,3,1,0:T(8,128)(2,1)S(1)}, u32[]{:S(2)}, u32[]{:S(2)}) collective-permute-start(bf16[1,2,512,256]{2,3,1,0:T(8,128)(2,1)} %bitcast.49), channel_id=1, source_target_pairs={{0,8},{4,12},{8,16},{12,20},{16,24},{20,28},{1,9},{5,13},{9,17},{1... | collective-permute-start | bytes 1572872 | tf_op jit(solution)/shard_map/ppermute | solution.py:13
Sparse Core Ops, SparseCore 0:
  9.7 48.3 all-gather.3
Sparse Core Ops, SparseCore 1:
  76.4 23.4 all-gather.7
  127.7 26.0 all-gather.5
where the time goes:
time: 165 us; the launch traced here: 164 us
  waiting for transfers between devices  88.4 us (54%)
  starting transfers between devices  23.3 us (14%)
  between operations  15 us (9%)
  matrix products  14.1 us (9%)
  other arithmetic  13.4 us (8%)
  local copies, waits for them, and re-layouts  10.2 us (6%)
    all_gather x1, waiting for transfers between devices, local(): gathered = lax.all_gather(layer_input, 'head', axis=2, tiled=True)  50 us
    all_gather x1, waiting for transfers between devices, local(): full_ctx = lax.all_gather(context, 'head', axis=2, tiled=True)  26.1 us
    ppermute x3, starting transfers between devices, passed_along(): return lax.ppermute(block, axis, route)  23.2 us
    ppermute x3, waiting for transfers between devices, passed_along(): return lax.ppermute(block, axis, route)  11.5 us
    unnamed x11, local copies, waits for them, and re-layouts  5.9 us
    dot_general x1, matrix products, attend(): jnp.einsum('bhqk,bkhd->bqhd', weights, value_heads, preferred_element_typ...  5.18 us
    unnamed x2, other arithmetic  5.02 us
    sub x1, matrix products, attend(): exponent = jnp.exp(scores - highest)  3.83 us
  transfers between devices with their start and end apart: 6, of which 5 were waited for; matrix products, arithmetic and copies ran while one was open for 18% of the time, Pallas kernels for 0%

commit v1 on v0

--- a/solution.py
+++ b/solution.py
@@ -56,7 +56,31 @@
 
 
 def local(layer_input, w_qkv, comp_weight, w_out):
-    gathered = lax.all_gather(layer_input, "head", axis=2, tiled=True)
+    outer = lax.axis_size("head")
+    piece_next = lax.axis_index("head")
+    piece_out, y, e_next = (outer, piece_next, layer_input.shape[2])
+    steps_seen = []
+    for k in range(piece_out):
+        steps_seen.append((k, (k + 1) % piece_out))
+    entries = []
+    for k in range(piece_out):
+        entries.append((k, (k - 1) % piece_out))
+    gathered = jnp.zeros(
+        (*layer_input.shape[:2], piece_out * e_next, *layer_input.shape[3:]), layer_input.dtype
+    )
+    gathered = lax.dynamic_update_slice_in_dim(gathered, layer_input, y * e_next, axis=2)
+    current_block = all_values = layer_input
+    step_out = piece_out // 2
+    for it in range(1, step_out + 1):
+        current_block = lax.ppermute(current_block, "head", steps_seen)
+        gathered = lax.dynamic_update_slice_in_dim(
+            gathered, current_block, (y - it) % piece_out * e_next, axis=2
+        )
+        if it < piece_out - step_out:
+            all_values = lax.ppermute(all_values, "head", entries)
+            gathered = lax.dynamic_update_slice_in_dim(
+                gathered, all_values, (y + it) % piece_out * e_next, axis=2
+            )
     normed = layer_norm(gathered.astype(jnp.float32)).astype(jnp.bfloat16)
     projected = jnp.einsum("bld,dkc->bklc", normed, w_qkv, preferred_element_type=jnp.float32)
     projected = projected.astype(jnp.bfloat16)

time: 165 us -> 152 us (0.921)
  waiting for transfers between devices: 88.4 us -> 69.2 us
  starting transfers between devices: 23.3 us -> 28.2 us
  local copies, waits for them, and re-layouts: 10.2 us -> 14.7 us
  other arithmetic: 13.4 us -> 11.7 us
    all_gather x1 -> x0, waiting for transfers between devices: 50 us -> none  [local(): gathered = lax.all_gather(layer_input, 'head', axis=2, tiled=True)]
    ppermute x0 -> x3, waiting for transfers between devices: none -> 31.1 us  [the longest x2 23.6 us: local(): current_block = lax.ppermute(current_block, 'head', steps_seen)]
    ppermute x0 -> x3, starting transfers between devices: none -> 5.08 us  [the longest x2 3.05 us: local(): current_block = lax.ppermute(current_block, 'head', steps_seen)]
    dynamic_update_slice x0 -> x4, local copies, waits for them, and re-layouts: none -> 4.42 us  [the longest x2 2.21 us: local(): lax.dynamic_update_slice_in_dim(gathered, current_block, (y - it) % piece...]
    reduce_sum x1, other arithmetic: 2.09 us -> 0.35 us  [layer_norm(): center_mean = jnp.mean(values, axis=-1, keepdims=True)]
    unnamed x11 -> x9, local copies, waits for them, and re-layouts: 5.9 us -> 5.79 us
  transfers between devices with their start and end apart: 6 -> 8, of which waited for: 5 -> 7; matrix products, arithmetic and copies ran while one was open for 18% -> 21% of each run, Pallas kernels for 0% -> 0%
where the time goes in v1:
time: 152 us; the launch traced here: 151 us
  waiting for transfers between devices  69.2 us (46%)
  starting transfers between devices  28.2 us (19%)
  local copies, waits for them, and re-layouts  14.7 us (10%)
  matrix products  14.1 us (9%)
  between operations  13.6 us (9%)
  other arithmetic  11.7 us (8%)
    all_gather x1, waiting for transfers between devices, local(): full_ctx = lax.all_gather(context, 'head', axis=2, tiled=True)  27.4 us
    ppermute x2, waiting for transfers between devices, local(): current_block = lax.ppermute(current_block, 'head', steps_seen)  23.6 us
    ppermute x3, starting transfers between devices, passed_along(): return lax.ppermute(block, axis, route)  23.1 us
    ppermute x3, waiting for transfers between devices, passed_along(): return lax.ppermute(block, axis, route)  10.6 us
    ppermute x1, waiting for transfers between devices, local(): all_values = lax.ppermute(all_values, 'head', entries)  7.53 us
    unnamed x9, local copies, waits for them, and re-layouts  5.79 us
    dot_general x1, matrix products, attend(): jnp.einsum('bhqk,bkhd->bqhd', weights, value_heads, preferred_element_typ...  5.18 us
    unnamed x2, other arithmetic  5.02 us
  transfers between devices with their start and end apart: 8, of which 7 were waited for; matrix products, arithmetic and copies ran while one was open for 21% of the time, Pallas kernels for 0%

profile of v1, /device:TPU:0, one launch (start us, length us, event | category | flops | bytes accessed | tf_op | source)
XLA Modules:
  0.0 151.5 jit_solution(6892430583196126167)
XLA Ops:
  6.5 0.0 copy-start
  6.5 0.0 all-gather.5.cloned.1.call-start
  6.5 3.1 %collective-permute-start = (bf16[1,512,512]{2,1,0:T(8,128)(2,1)}, bf16[1,512,512]{2,1,0:T(8,128)(2,1)}, u32[]{:S(2)}, u32[]{:S(2)}) collective-permute-start(bf16[1,512,512]{2,1,0:T(8,128)(2,1)} %param.4), channel_id=1, source_target_pairs={{0,1},{1,2},{2,3},{3,0},{4,5},{5,6},{6,7},{7,4},{8,9},{9,10},{10,1... | collective-permute-start | bytes 1572872 | tf_op jit(solution)/shard_map/ppermute | solution.py:75
  9.6 2.0 %collective-permute-start.1 = (bf16[1,512,512]{2,1,0:T(8,128)(2,1)}, bf16[1,512,512]{2,1,0:T(8,128)(2,1)}, u32[]{:S(2)}, u32[]{:S(2)}) collective-permute-start(bf16[1,512,512]{2,1,0:T(8,128)(2,1)} %param.4), channel_id=1, source_target_pairs={{0,3},{1,0},{2,1},{3,2},{4,7},{5,4},{6,5},{7,6},{8,11},{9,8},{10,9... | collective-permute-start | bytes 1572872 | tf_op jit(solution)/shard_map/ppermute | solution.py:80
  11.6 13.1 %collective-permute-done = bf16[1,512,512]{2,1,0:T(8,128)(2,1)} collective-permute-done((bf16[1,512,512]{2,1,0:T(8,128)(2,1)}, bf16[1,512,512]{2,1,0:T(8,128)(2,1)}, u32[]{:S(2)}, u32[]{:S(2)}) %collective-permute-start) | collective-permute-done | bytes 524320 | tf_op jit(solution)/shard_map/ppermute | solution.py:75
  24.8 0.0 collective-permute-start.2
  24.8 0.2 broadcast_in_dim.14
  25.0 1.1 constant_dynamic-update-slice_fusion.3
  26.1 1.1 constant_dynamic-update-slice_fusion.2
  27.2 7.5 %collective-permute-done.1 = bf16[1,512,512]{2,1,0:T(8,128)(2,1)} collective-permute-done((bf16[1,512,512]{2,1,0:T(8,128)(2,1)}, bf16[1,512,512]{2,1,0:T(8,128)(2,1)}, u32[]{:S(2)}, u32[]{:S(2)}) %collective-permute-start.1) | collective-permute-done | bytes 524320 | tf_op jit(solution)/shard_map/ppermute | solution.py:80
  34.8 1.1 constant_dynamic-update-slice_fusion.1
  35.9 10.5 %collective-permute-done.2 = bf16[1,512,512]{2,1,0:T(8,128)(2,1)} collective-permute-done((bf16[1,512,512]{2,1,0:T(8,128)(2,1)}, bf16[1,512,512]{2,1,0:T(8,128)(2,1)}, u32[]{:S(2)}, u32[]{:S(2)}) %collective-permute-start.2) | collective-permute-done | bytes 524320 | tf_op jit(solution)/shard_map/ppermute | solution.py:75
  46.4 1.1 constant_dynamic-update-slice_fusion
  47.5 0.4 convert_reduce_fusion
  47.8 0.7 fusion.4
  48.5 0.0 copy-done
  48.6 0.0 copy-start.3
  48.6 2.0 %fusion.21 = bf16[1,3,512,256]{2,3,1,0:T(8,128)(2,1)S(1)} fusion(bf16[2048,3,256]{2,0,1:T(8,128)(2,1)S(1)} %copy-done, bf16[1,512,2048]{2,1,0:T(8,128)(2,1)S(1)} %constant_dynamic-update-slice_fusion, f32[512]{0:T(512)S(1)} %add_rsqrt_fusion, f32[512]{0:T(512)S(1)} %broadcast_multiply_fusion), kind=kOutput, calls=%fused_computation.29 | convolution fusion | flops 1615200256 | bytes 6033408 | tf_op jit(solution)/shard_map/bld,dkc->bklc/dot_general | solution.py:85
  50.6 0.0 copy-start.2
  50.6 0.0 copy-start.1
  50.6 0.8 copy-done.1
  51.5 2.1 %collective-permute-start.3 = (bf16[1,2,512,256]{2,3,1,0:T(8,128)(2,1)S(1)}, bf16[1,2,512,256]{2,3,1,0:T(8,128)(2,1)}, u32[]{:S(2)}, u32[]{:S(2)}) collective-permute-start(bf16[1,2,512,256]{2,3,1,0:T(8,128)(2,1)S(1)} %slice.16), channel_id=1, source_target_pairs={{0,4},{4,8},{8,12},{12,16},{16,20},{20,24},{24,28},{1,5},{5,9},{9,... | collective-permute-start | bytes 1572872 | tf_op jit(solution)/shard_map/ppermute | solution.py:13
  53.6 0.8 collective-permute-done.3
  54.4 0.0 copy-done.2
  54.4 9.4 %collective-permute-start.4 = (bf16[1,2,512,256]{2,3,1,0:T(8,128)(2,1)}, bf16[1,2,512,256]{2,3,1,0:T(8,128)(2,1)}, u32[]{:S(2)}, u32[]{:S(2)}) collective-permute-start(bf16[1,2,512,256]{2,3,1,0:T(8,128)(2,1)} %collective-permute-done.3), channel_id=1, source_target_pairs={{0,4},{4,8},{8,12},{12,16},{16,20},{20,24},{24,28},{1,5},{5,9},{9,... | collective-permute-start | bytes 1572872 | tf_op jit(solution)/shard_map/ppermute | solution.py:13
  63.8 0.0 all-gather.5.cloned.1.call-update
  63.8 0.0 all-gather.3.cloned.1.call-start
  63.9 0.0 copy-done.3
  63.9 0.9 collective-permute-done.4
  64.8 2.6 %pad_maximum_fusion.1 = bf16[1,2,1536,256]{2,3,1,0:T(8,128)(2,1)} fusion(bf16[1,2,512,256]{2,3,1,0:T(8,128)(2,1)} %copy-done.1, bf16[1,2,512,256]{2,3,1,0:T(8,128)(2,1)} %collective-permute-done.3, bf16[1,2,512,256]{2,3,1,0:T(8,128)(2,1)} %collective-permute-done.4), kind=kLoop, calls=%fused_computation.25 | loop fusion | flops 4718592 | bytes 3145728 | tf_op jit(solution)/shard_map/concatenate | solution.py:91
  67.5 4.9 %copy.23 = bf16[1,2,1536,256]{3,1,2,0:T(2,128)(2,1)} copy(bf16[1,2,1536,256]{2,3,1,0:T(8,128)(2,1)} %pad_maximum_fusion.1) | data formatting | bytes 3145728
  72.4 5.0 %multiply_reduce_fusion = bf16[2,256,512]{1,0,2:T(2,128)(2,1)} fusion(bf16[2,256,3,512]{1,0,2,3:T(2,128)(2,1)} %bitcast.45, f32[2,256,3]{1,0,2:T(2,128)S(1)} %bitcast_convert_fusion), kind=kLoop, calls=%fused_computation.11 | loop fusion | flops 2097152 | bytes 2103296
  77.4 2.0 %copy.20 = bf16[2,256,512]{2,1,0:T(8,128)(2,1)} copy(bf16[2,256,512]{1,0,2:T(2,128)(2,1)} %multiply_reduce_fusion) | data formatting | bytes 1048576 | tf_op jit(solution)/shard_map/bkltc,tkc->bklc/dot_general | solution.py:26
  79.4 11.6 %collective-permute-start.5 = (bf16[1,2,512,256]{2,3,1,0:T(8,128)(2,1)}, bf16[1,2,512,256]{2,3,1,0:T(8,128)(2,1)S(1)}, u32[]{:S(2)}, u32[]{:S(2)}) collective-permute-start(bf16[1,2,512,256]{2,3,1,0:T(8,128)(2,1)} %bitcast.49), channel_id=1, source_target_pairs={{0,8},{4,12},{8,16},{12,20},{16,24},{20,28},{1,9},{5,13},{9,17},{1... | collective-permute-start | bytes 1572872 | tf_op jit(solution)/shard_map/ppermute | solution.py:13
  91.1 1.6 %fusion.10 = pred[512,1536]{1,0:T(8,128)(4,1)} fusion(s32[1536]{0:T(1024)S(1)} %iota_add_fusion, pred[1536]{0:T(1024)(128)(4,1)S(1)} %get-tuple-element.8, pred[1536]{0:T(1024)(128)(4,1)S(1)} %fusion.31, pred[1536]{0:T(1024)(128)(4,1)S(1)} %get-tuple-element.7), kind=kLoop, calls=%fused_computation.17 | loop fusion | flops 3145728 | bytes 797184 | tf_op jit(solution)/shard_map/or | solution.py:36
  92.7 1.0 slice.18
  93.7 8.8 %collective-permute-done.5 = bf16[1,2,512,256]{2,3,1,0:T(8,128)(2,1)S(1)} collective-permute-done((bf16[1,2,512,256]{2,3,1,0:T(8,128)(2,1)}, bf16[1,2,512,256]{2,3,1,0:T(8,128)(2,1)S(1)}, u32[]{:S(2)}, u32[]{:S(2)}) %collective-permute-start.5) | collective-permute-done | bytes 524320 | tf_op jit(solution)/shard_map/ppermute | solution.py:13
  102.5 1.3 pad_maximum_fusion
  103.8 1.3 fusion.39
  105.1 3.8 %fusion.40 = f32[2,512]{1,0:T(2,128)S(1)} fusion(pred[512,1536]{1,0:T(8,128)(4,1)} %fusion.10, bf16[512,2,128]{0,2,1:T(8,128)(2,1)S(1)} %bitcast.50, bf16[1536,2,128]{0,2,1:T(8,128)(2,1)} %bitcast.46), kind=kOutput, calls=%fused_computation.57 | convolution fusion | flops 408946176 | bytes 1839104 | tf_op jit(solution)/shard_map/sub | solution.py:52
  108.9 5.2 %fusion.25 = bf16[2,128,512]{2,1,0:T(8,128)(2,1)} fusion(bf16[1536,2,128]{0,2,1:T(8,128)(2,1)} %bitcast.48, f32[2,512]{1,0:T(2,128)S(1)} %fusion.40, pred[512,1536]{1,0:T(8,128)(4,1)} %fusion.10, bf16[512,2,128]{0,2,1:T(8,128)(2,1)S(1)} %bitcast.51, bf16[1536,2,128]{0,2,1:T(8,128)(2,1)} %bitcast.47), kind=kOutput, calls=%fused_computation.32 | convolution fusion | flops 813304320 | bytes 2887680 | tf_op jit(solution)/shard_map/bhqk,bkhd->bqhd/dot_general | solution.py:54
  114.1 0.0 all-gather.3.cloned.1.call-update
  114.1 0.0 all-gather.5.cloned.1.call-done
  114.2 27.4 %all-gather.3.cloned.1.call-done = bf16[1,512,1024]{1,2,0:T(8,128)(2,1)} async-done(((bf16[1,512,256]{1,2,0:T(8,128)(2,1)}), bf16[1,512,1024]{1,2,0:T(8,128)(2,1)}) %all-gather.3.cloned.1.call-update) | async-done | bytes 1048592 | tf_op jit(solution)/shard_map/all_gather | solution.py:96
  141.6 3.1 %fusion.24 = bf16[1,512,512]{2,1,0:T(8,128)(2,1)} fusion(bf16[1024,512]{1,0:T(8,128)(2,1)} %all-gather.5.cloned.1.call-done, bf16[1,512,1024]{1,2,0:T(8,128)(2,1)} %all-gather.3.cloned.1.call-done), kind=kOutput, calls=%fused_computation.31 | convolution fusion | flops 537133056 | bytes 2621440 | tf_op jit(solution)/shard_map/blr,rc->blc/dot_general | solution.py:98
  (7 shorter events, 0.1 us)
Async XLA Ops:
  6.5 42.0 %copy-start = (bf16[2048,3,256]{2,0,1:T(8,128)(2,1)S(1)}, bf16[2048,3,256]{2,0,1:T(8,128)(2,1)}, u32[]{:S(2)}) copy-start(bf16[2048,3,256]{2,0,1:T(8,128)(2,1)} %param.5) | copy-start | bytes 9437188
  6.5 107.6 %all-gather.5.cloned.1.call-start = ((), (), s32[]{:S(2)}) async-start(), calls=%async_computation.1 | async-start | bytes 1179648 | tf_op jit(solution)/shard_map/all_gather | solution.py:97
  6.5 18.2 %collective-permute-start = (bf16[1,512,512]{2,1,0:T(8,128)(2,1)}, bf16[1,512,512]{2,1,0:T(8,128)(2,1)}, u32[]{:S(2)}, u32[]{:S(2)}) collective-permute-start(bf16[1,512,512]{2,1,0:T(8,128)(2,1)} %param.4), channel_id=1, source_target_pairs={{0,1},{1,2},{2,3},{3,0},{4,5},{5,6},{6,7},{7,4},{8,9},{9,10},{10,1... | collective-permute-start | bytes 1572872 | tf_op jit(solution)/shard_map/ppermute | solution.py:75
  9.6 25.2 %collective-permute-start.1 = (bf16[1,512,512]{2,1,0:T(8,128)(2,1)}, bf16[1,512,512]{2,1,0:T(8,128)(2,1)}, u32[]{:S(2)}, u32[]{:S(2)}) collective-permute-start(bf16[1,512,512]{2,1,0:T(8,128)(2,1)} %param.4), channel_id=1, source_target_pairs={{0,3},{1,0},{2,1},{3,2},{4,7},{5,4},{6,5},{7,6},{8,11},{9,8},{10,9... | collective-permute-start | bytes 1572872 | tf_op jit(solution)/shard_map/ppermute | solution.py:80
  24.8 21.6 %collective-permute-start.2 = (bf16[1,512,512]{2,1,0:T(8,128)(2,1)}, bf16[1,512,512]{2,1,0:T(8,128)(2,1)}, u32[]{:S(2)}, u32[]{:S(2)}) collective-permute-start(bf16[1,512,512]{2,1,0:T(8,128)(2,1)} %collective-permute-done), channel_id=1, source_target_pairs={{0,1},{1,2},{2,3},{3,0},{4,5},{5,6},{6,7},{7,4},{8,9},{9,10},{10,1... | collective-permute-start | bytes 1572872 | tf_op jit(solution)/shard_map/ppermute | solution.py:75
  48.6 15.3 %copy-start.3 = (bf16[3,2,256]{2,1,0:T(2,128)(2,1)S(1)}, bf16[3,2,256]{2,1,0:T(2,128)(2,1)}, u32[]{:S(2)}) copy-start(bf16[3,2,256]{2,1,0:T(2,128)(2,1)} %param.6) | copy-start | bytes 9220
  50.6 3.8 %copy-start.2 = (bf16[1,3,512,256]{2,3,1,0:T(8,128)(2,1)}, bf16[1,3,512,256]{2,3,1,0:T(8,128)(2,1)S(1)}, u32[]{:S(2)}) copy-start(bf16[1,3,512,256]{2,3,1,0:T(8,128)(2,1)S(1)} %fusion.21) | copy-start | bytes 2359300
  50.6 0.8 copy-start.1
  51.5 2.9 %collective-permute-start.3 = (bf16[1,2,512,256]{2,3,1,0:T(8,128)(2,1)S(1)}, bf16[1,2,512,256]{2,3,1,0:T(8,128)(2,1)}, u32[]{:S(2)}, u32[]{:S(2)}) collective-permute-start(bf16[1,2,512,256]{2,3,1,0:T(8,128)(2,1)S(1)} %slice.16), channel_id=1, source_target_pairs={{0,4},{4,8},{8,12},{12,16},{16,20},{20,24},{24,28},{1,5},{5,9},{9,... | collective-permute-start | bytes 1572872 | tf_op jit(solution)/shard_map/ppermute | solution.py:13
  54.4 10.4 %collective-permute-start.4 = (bf16[1,2,512,256]{2,3,1,0:T(8,128)(2,1)}, bf16[1,2,512,256]{2,3,1,0:T(8,128)(2,1)}, u32[]{:S(2)}, u32[]{:S(2)}) collective-permute-start(bf16[1,2,512,256]{2,3,1,0:T(8,128)(2,1)} %collective-permute-done.3), channel_id=1, source_target_pairs={{0,4},{4,8},{8,12},{12,16},{16,20},{20,24},{24,28},{1,5},{5,9},{9,... | collective-permute-start | bytes 1572872 | tf_op jit(solution)/shard_map/ppermute | solution.py:13
  63.8 77.8 %all-gather.3.cloned.1.call-start = ((), (), s32[]{:S(2)}) async-start(), calls=%async_computation | async-start | bytes 1310720 | tf_op jit(solution)/shard_map/all_gather | solution.py:96
  79.4 23.1 %collective-permute-start.5 = (bf16[1,2,512,256]{2,3,1,0:T(8,128)(2,1)}, bf16[1,2,512,256]{2,3,1,0:T(8,128)(2,1)S(1)}, u32[]{:S(2)}, u32[]{:S(2)}) collective-permute-start(bf16[1,2,512,256]{2,3,1,0:T(8,128)(2,1)} %bitcast.49), channel_id=1, source_target_pairs={{0,8},{4,12},{8,16},{12,20},{16,24},{20,28},{1,9},{5,13},{9,17},{1... | collective-permute-start | bytes 1572872 | tf_op jit(solution)/shard_map/ppermute | solution.py:13
Sparse Core Ops, SparseCore 0:
  63.9 24.0 all-gather.4
  114.2 27.2 all-gather.2
